TPU v7x, 32 devices: a whole 2x2x4 slice. The times are simulated.
32 devices in a mesh: dp: 8 (over z, x), mp: 4 (over y, core).
Axes of the slice: x: 2, y: 2, z: 4, core: 2. Of those that a mesh axis runs over, the one named last changes fastest.
Arguments:
- rows: float32 [16384, 1280], P(('dp', 'mp')), may hold values from -6 to 6
- lengths: int32 [256], P('dp'), may hold values from 1 to 64, as said below
- freq_class: int32 [256], P(('dp', 'mp')), may hold values from 0 to 2
- freq_table: float32 [3, 1280], replicated, may hold values from -3 to 3
- gain_attn: float32 [1280], replicated, may hold values from 0.5 to 1.5
- gain_mlp: float32 [1280], replicated, may hold values from 0.5 to 1.5
- w_qkv: float32 [3, 1280, 1280], P(None, None, 'mp'), may hold values from -0.15625 to 0.15625
- w_out: float32 [1280, 1280], P('mp'), may hold values from -0.5 to 0.5
- w_gate_up: float32 [2, 1280, 5120], P(None, None, 'mp'), may hold values from -0.15625 to 0.15625
- w_down: float32 [5120, 1280], P('mp'), may hold values from -0.15625 to 0.15625
- cotangent: float32 [16384, 1280], P(('dp', 'mp')), may hold values from -6 to 6
Outputs:
- output: float32 [16384, 1280], P(('dp', 'mp'))
- grad_rows: float32 [16384, 1280], P(('dp', 'mp'))
- grad_qkv: float32 [3, 1280, 1280], P(None, None, 'mp')
- grad_out: float32 [1280, 1280], P('mp')
- grad_gate_up: float32 [2, 1280, 5120], P(None, None, 'mp')
- grad_down: float32 [5120, 1280], P('mp')
- grad_gain_attn: float32 [1280], replicated
- grad_gain_mlp: float32 [1280], replicated
- grad_table: float32 [3, 1280], replicated
Inputs may be any that keep to these rules, and one draw needn't show every extreme that they name: `lengths`: the valid patches of a series are the last of its 64 slots; some series has all 64, and some only one.
All inputs are finite; a program needn't handle non-finite values.
Results may differ from a plain program's by a relative error of at most 0.02.
Values may be sent and summed in bfloat16 or wider, within the bound.
A program may use at most 256 MiB of HBM per device.

v0:
```python
import jax
import jax.numpy as jnp
from jax import lax
from jax.sharding import PartitionSpec as P

HS = 80
NFREQ = 3
SEQ = 64
EPSILON = 1e-06
NEGATIVE = -1e30
HIGHEST = lax.Precision.HIGHEST


def rotate(values, cosines, sines):
    half_width = values.shape[-1] // 2
    first_half = values[..., :half_width]
    second_half = values[..., half_width:]
    return jnp.concatenate(
        [first_half * cosines - second_half * sines, second_half * cosines + first_half * sines], -1
    )


def series_tables(series_lengths):
    places = jnp.arange(SEQ, dtype=jnp.int32)
    starts = SEQ - series_lengths
    valid_mask = places[None, :] >= starts[:, None]
    positions = (places[None, :] - starts[:, None]).astype(jnp.float32)
    frequency = 10000.0 ** (-2.0 * jnp.arange(HS // 2, dtype=jnp.float32) / HS)
    angles = positions[:, :, None] * frequency[None, None, :]
    return (valid_mask, jnp.cos(angles)[:, :, None, :], jnp.sin(angles)[:, :, None, :])


def allowed_pairs(valid_mask):
    places = jnp.arange(SEQ, dtype=jnp.int32)
    causal = places[:, None] >= places[None, :]
    itself = places[:, None] == places[None, :]
    return causal[None, None] & (valid_mask[:, None, None, :] | itself[None, None])


def norm_forward(values, gain):
    inverse = lax.rsqrt(jnp.mean(values * values, -1, keepdims=True) + EPSILON)
    return ((values * inverse * gain).astype(jnp.bfloat16), inverse)


def norm_backward(values, inverse, gain, grad_normed):
    normal = values * inverse
    grad_gain = jnp.sum(grad_normed * normal, 0)
    scaled = grad_normed * gain
    grad_values = inverse * (scaled - normal * jnp.mean(scaled * normal, -1, keepdims=True))
    return (grad_values, grad_gain)


def attention_scores(queries, keys, allowed):
    raw_scores = jnp.einsum("sihe,sjhe->shij", queries, keys, preferred_element_type=jnp.float32)
    return jnp.where(allowed, raw_scores * HS ** (-0.5), NEGATIVE)


def body(
    rows,
    lengths,
    freq_class,
    freq_table,
    gain_attn,
    gain_mlp,
    w_qkv,
    w_out,
    w_gate_up,
    w_down,
    cotangent,
):
    local_rows = rows.shape[0]
    mp_index = lax.axis_index("mp")
    series_count = lengths.shape[0]
    group_rows = series_count * SEQ
    heads_width = w_out.shape[0]
    head_count = heads_width // HS
    valid_mask, cosines, sines = series_tables(lengths)
    allowed = allowed_pairs(valid_mask)
    flat_valid = valid_mask.reshape(group_rows).astype(jnp.float32)
    mine_valid = lax.dynamic_slice_in_dim(flat_valid, mp_index * local_rows, local_rows)[:, None]
    classes = jnp.repeat(freq_class, SEQ)
    onehot = (classes[:, None] == jnp.arange(NFREQ, dtype=jnp.int32)[None, :]).astype(jnp.float32)
    start_rows = rows + jnp.dot(onehot, freq_table, precision=HIGHEST)
    normed_mine, inverse_attn = norm_forward(start_rows, gain_attn)
    normed = lax.all_gather(normed_mine, "mp", axis=0, tiled=True)
    qkv_low = w_qkv.astype(jnp.bfloat16)
    projected = jnp.einsum("td,cdf->ctf", normed, qkv_low, preferred_element_type=jnp.float32)
    projected = projected.reshape(3, series_count, SEQ, head_count, HS)
    queries = rotate(projected[0], cosines, sines).astype(jnp.bfloat16)
    keys = rotate(projected[1], cosines, sines).astype(jnp.bfloat16)
    values = projected[2].astype(jnp.bfloat16)
    scores = attention_scores(queries, keys, allowed)
    row_max = jnp.max(scores, -1, keepdims=True)
    exponent = jnp.exp(scores - row_max)
    row_total = jnp.sum(exponent, -1, keepdims=True)
    log_total = row_max + jnp.log(row_total)
    attention = (exponent / row_total).astype(jnp.bfloat16)
    mixed = jnp.einsum("shij,sjhe->sihe", attention, values, preferred_element_type=jnp.float32)
    mixed = mixed.reshape(group_rows, heads_width).astype(jnp.bfloat16)
    out_low = w_out.astype(jnp.bfloat16)
    attn_part = jnp.dot(mixed, out_low, preferred_element_type=jnp.float32)
    after_attn = start_rows + lax.psum_scatter(
        attn_part.astype(jnp.bfloat16), "mp", scatter_dimension=0, tiled=True
    ).astype(jnp.float32)
    normed_mlp_mine, inverse_mlp = norm_forward(after_attn, gain_mlp)
    normed_mlp = lax.all_gather(normed_mlp_mine, "mp", axis=0, tiled=True)
    gate_up_low = w_gate_up.astype(jnp.bfloat16)
    gate_up = jnp.einsum("td,cdf->ctf", normed_mlp, gate_up_low, preferred_element_type=jnp.float32)
    gate_pre = gate_up[0]
    up_pre = gate_up[1]
    sigmoid_gate = jax.nn.sigmoid(gate_pre)
    activated = gate_pre * sigmoid_gate
    hidden = (activated * up_pre).astype(jnp.bfloat16)
    down_low = w_down.astype(jnp.bfloat16)
    mlp_part = jnp.dot(hidden, down_low, preferred_element_type=jnp.float32)
    output = after_attn + lax.psum_scatter(
        mlp_part.astype(jnp.bfloat16), "mp", scatter_dimension=0, tiled=True
    ).astype(jnp.float32)
    grad_output = cotangent * mine_valid
    grad_down_in = lax.all_gather(grad_output.astype(jnp.bfloat16), "mp", axis=0, tiled=True)
    grad_down = jnp.einsum("tf,td->fd", hidden, grad_down_in, preferred_element_type=jnp.float32)
    grad_hidden = jnp.einsum(
        "td,fd->tf", grad_down_in, down_low, preferred_element_type=jnp.float32
    )
    grad_gate = grad_hidden * up_pre * (sigmoid_gate * (1.0 + gate_pre * (1.0 - sigmoid_gate)))
    grad_up = grad_hidden * activated
    grad_pre = jnp.stack([grad_gate, grad_up]).astype(jnp.bfloat16)
    grad_gate_up = jnp.einsum(
        "td,ctf->cdf", normed_mlp, grad_pre, preferred_element_type=jnp.float32
    )
    mlp_back_part = jnp.einsum(
        "ctf,cdf->td", grad_pre, gate_up_low, preferred_element_type=jnp.float32
    )
    grad_normed_mlp = lax.psum_scatter(
        mlp_back_part.astype(jnp.bfloat16), "mp", scatter_dimension=0, tiled=True
    ).astype(jnp.float32)
    grad_rows_mlp, grad_gain_mlp = norm_backward(after_attn, inverse_mlp, gain_mlp, grad_normed_mlp)
    grad_after = grad_output + grad_rows_mlp
    grad_attn_in = lax.all_gather(grad_after.astype(jnp.bfloat16), "mp", axis=0, tiled=True)
    grad_out = jnp.einsum("tf,td->fd", mixed, grad_attn_in, preferred_element_type=jnp.float32)
    grad_mixed = jnp.einsum("td,fd->tf", grad_attn_in, out_low, preferred_element_type=jnp.float32)
    grad_mixed = grad_mixed.astype(jnp.bfloat16).reshape(series_count, SEQ, head_count, HS)
    attention_again = jnp.exp(attention_scores(queries, keys, allowed) - log_total)
    grad_attention = jnp.einsum(
        "sihe,sjhe->shij", grad_mixed, values, preferred_element_type=jnp.float32
    )
    grad_values = jnp.einsum(
        "shij,sihe->sjhe",
        attention_again.astype(jnp.bfloat16),
        grad_mixed,
        preferred_element_type=jnp.float32,
    )
    row_dot = jnp.sum(attention_again * grad_attention, -1, keepdims=True)
    grad_scores = (attention_again * (grad_attention - row_dot)).astype(jnp.bfloat16)
    grad_queries = jnp.einsum(
        "shij,sjhe->sihe", grad_scores, keys, preferred_element_type=jnp.float32
    ) * HS ** (-0.5)
    grad_keys = jnp.einsum(
        "shij,sihe->sjhe", grad_scores, queries, preferred_element_type=jnp.float32
    ) * HS ** (-0.5)
    grad_projected = jnp.stack(
        [rotate(grad_queries, cosines, -sines), rotate(grad_keys, cosines, -sines), grad_values]
    )
    grad_projected = grad_projected.reshape(3, group_rows, heads_width).astype(jnp.bfloat16)
    grad_qkv = jnp.einsum("td,ctf->cdf", normed, grad_projected, preferred_element_type=jnp.float32)
    attn_back_part = jnp.einsum(
        "ctf,cdf->td", grad_projected, qkv_low, preferred_element_type=jnp.float32
    )
    grad_normed = lax.psum_scatter(
        attn_back_part.astype(jnp.bfloat16), "mp", scatter_dimension=0, tiled=True
    ).astype(jnp.float32)
    grad_rows_attn, grad_gain_attn = norm_backward(start_rows, inverse_attn, gain_attn, grad_normed)
    grad_rows = grad_after + grad_rows_attn
    grad_table = jnp.dot(onehot.T, grad_rows, precision=HIGHEST)
    grad_gain_attn, grad_gain_mlp, grad_table, token_total = lax.psum(
        (grad_gain_attn, grad_gain_mlp, grad_table, jnp.sum(mine_valid)), ("dp", "mp")
    )
    grad_qkv, grad_out, grad_gate_up, grad_down = (
        lax.psum(grad_qkv.astype(jnp.bfloat16), "dp").astype(jnp.float32),
        lax.psum(grad_out.astype(jnp.bfloat16), "dp").astype(jnp.float32),
        lax.psum(grad_gate_up.astype(jnp.bfloat16), "dp").astype(jnp.float32),
        lax.psum(grad_down.astype(jnp.bfloat16), "dp").astype(jnp.float32),
    )
    root_scale = lax.rsqrt(token_total)
    return (
        output,
        grad_rows,
        grad_qkv * root_scale,
        grad_out * root_scale,
        grad_gate_up * root_scale,
        grad_down * root_scale,
        grad_gain_attn * root_scale,
        grad_gain_mlp * root_scale,
        grad_table * root_scale,
    )


def solution(mesh):
    return jax.shard_map(
        body,
        mesh=mesh,
        in_specs=(
            P(("dp", "mp"), None),
            P("dp"),
            P(("dp", "mp")),
            P(),
            P(),
            P(),
            P(None, None, "mp"),
            P("mp", None),
            P(None, None, "mp"),
            P("mp", None),
            P(("dp", "mp"), None),
        ),
        out_specs=(
            P(("dp", "mp"), None),
            P(("dp", "mp"), None),
            P(None, None, "mp"),
            P("mp", None),
            P(None, None, "mp"),
            P("mp", None),
            P(),
            P(),
            P(),
        ),
        check_vma=False,
    )
```

profile of v0, /device:TPU:0, one launch (start us, length us, event | category | flops | bytes accessed | tf_op | source)
XLA Modules:
  0.0 1067.2 jit_solution(17084121526547978977)
XLA Ops:
  8.1 3.2 multiply_reduce_fusion.2
  13.6 5.8 fusion.48
  19.4 36.9 %all-gather.5.cloned.1.call-done = bf16[2048,1280]{1,0:T(8,128)(2,1)} async-done(((bf16[512,1280]{1,0:T(8,128)(2,1)}), bf16[2048,1280]{1,0:T(8,128)(2,1)}) %all-gather.5.cloned.1.call-update) | async-done | bytes 5242896 | tf_op jit(solution)/shard_map/all_gather | solution.py:85
  56.3 8.7 fusion.10
  69.2 4.9 reshape.176
  74.1 4.7 copy.39
  78.8 5.3 reshape.177
  84.1 5.5 fusion.62
  89.6 4.9 copy.73
  94.5 4.9 copy.72
  99.3 5.3 reshape.178
  104.7 5.5 fusion.63
  110.1 4.9 copy.75
  115.0 4.9 copy.74
  119.9 7.9 subtract_convert_fusion.3
  135.5 3.3 copy.41
  138.7 4.3 convert_element_type.131
  143.1 7.1 convolution_convert_fusion.2
  150.3 51.5 %reduce-scatter.5.cloned.1.call-done = bf16[512,1280]{1,0:T(8,128)(2,1)} async-done(((bf16[2048,1280]{1,0:T(8,128)(2,1)}), bf16[512,1280]{1,0:T(8,128)(2,1)}) %reduce-scatter.5.cloned.1.call-update) | async-done | bytes 1310736 | tf_op jit(solution)/shard_map/reduce_scatter | solution.py:102
  208.6 38.5 %all-gather.7.cloned.1.call-done = bf16[2048,1280]{1,0:T(8,128)(2,1)} async-done(((bf16[512,1280]{1,0:T(8,128)(2,1)}), bf16[2048,1280]{1,0:T(8,128)(2,1)}) %all-gather.7.cloned.1.call-update) | async-done | bytes 5242896 | tf_op jit(solution)/shard_map/all_gather | solution.py:106
  247.0 22.6 %convolution_bitcast_fusion = f32[2,2048,1280]{2,1,0:T(8,128)} fusion(bf16[2048,1280]{1,0:T(8,128)(2,1)} %all-gather.7.cloned.1.call-done, f32[2,1280,1280]{2,1,0:T(8,128)} %param.19), kind=kOutput, calls=%fused_computation.1 | convolution fusion | flops 13425049600 | bytes 39321600 | tf_op jit(solution)/shard_map/td,cdf->ctf/dot_general | solution.py:108
  269.6 20.0 %all-gather.9.cloned.1.call-done = bf16[2048,1280]{1,0:T(8,128)(2,1)} async-done(((bf16[512,1280]{1,0:T(8,128)(2,1)}), bf16[2048,1280]{1,0:T(8,128)(2,1)}) %all-gather.9.cloned.1.call-update) | async-done | bytes 5242896 | tf_op jit(solution)/shard_map/all_gather | solution.py:120
  289.6 21.7 %fusion.9 = (bf16[1,2048,1280]{2,1,0:T(8,128)(2,1)}, bf16[1,2048,1280]{2,1,0:T(8,128)(2,1)}, bf16[2048,1280]{1,0:T(8,128)(2,1)}) fusion(f32[2,2048,1280]{2,1,0:T(8,128)} %convolution_bitcast_fusion, bf16[2048,1280]{1,0:T(8,128)(2,1)} %all-gather.9.cloned.1.call-done, f32[1280,1280]{1,0:T(8,128)} %param.20), kind=kOutput, calls=%fused_computation.25 | convolution fusion | flops 6751846400 | bytes 48496640 | tf_op jit(solution)/shard_map/td,fd->tf/dot_general | solution.py:122
  311.2 21.7 %bitcast_convert_fusion.1 = bf16[2048,1280]{1,0:T(8,128)(2,1)} fusion(bf16[1,2048,1280]{2,1,0:T(8,128)(2,1)} %get-tuple-element.46, bf16[1,2048,1280]{2,1,0:T(8,128)(2,1)} %get-tuple-element.45, f32[2,1280,1280]{2,1,0:T(8,128)} %param.19), kind=kOutput, calls=%fused_computation.7 | convolution fusion | flops 13432913920 | bytes 28835840 | tf_op jit(solution)/shard_map/ctf,cdf->td/dot_general | solution.py:131
  333.0 12.4 %convolution_convert_fusion.1 = bf16[2048,1280]{1,0:T(8,128)(2,1)} fusion(bf16[2048,1280]{1,0:T(8,128)(2,1)} %get-tuple-element.47, f32[1280,1280]{1,0:T(8,128)} %param.20), kind=kOutput, calls=%fused_computation.14 | convolution fusion | flops 6715146240 | bytes 17039360 | tf_op jit(solution)/shard_map/dot_general | solution.py:115
  345.4 39.1 %reduce-scatter.9.cloned.1.call-done = bf16[512,1280]{1,0:T(8,128)(2,1)} async-done(((bf16[2048,1280]{1,0:T(8,128)(2,1)}), bf16[512,1280]{1,0:T(8,128)(2,1)}) %reduce-scatter.9.cloned.1.call-update) | async-done | bytes 1310736 | tf_op jit(solution)/shard_map/reduce_scatter | solution.py:134
  386.7 51.7 %reduce-scatter.7.cloned.1.call-done = bf16[512,1280]{1,0:T(8,128)(2,1)} async-done(((bf16[2048,1280]{1,0:T(8,128)(2,1)}), bf16[512,1280]{1,0:T(8,128)(2,1)}) %reduce-scatter.7.cloned.1.call-update) | async-done | bytes 1310736 | tf_op jit(solution)/shard_map/reduce_scatter | solution.py:116
  438.4 6.3 fusion.59
  444.8 40.5 %all-gather.11.cloned.1.call-done = bf16[2048,1280]{1,0:T(8,128)(2,1)} async-done(((bf16[512,1280]{1,0:T(8,128)(2,1)}), bf16[2048,1280]{1,0:T(8,128)(2,1)}) %all-gather.11.cloned.1.call-update) | async-done | bytes 5242896 | tf_op jit(solution)/shard_map/all_gather | solution.py:139
  485.3 4.9 convolution_convert_fusion.5
  490.2 4.0 reshape.179
  494.2 3.6 copy.43
  497.8 4.5 convert_bitcast_fusion
  509.9 4.7 subtract_convert_fusion
  517.1 5.0 copy.59
  525.2 5.0 copy.60
  533.0 4.7 pad_maximum_fusion.5
  537.7 5.0 copy.58
  550.5 9.9 bitcast_convert_fusion
  560.5 12.3 %convolution_convert_fusion.3 = bf16[1280,1280]{1,0:T(8,128)(2,1)} fusion(bf16[2048,1280]{1,0:T(8,128)(2,1)} %get-tuple-element.47, bf16[2048,1280]{1,0:T(8,128)(2,1)} %all-gather.9.cloned.1.call-done), kind=kOutput, calls=%fused_computation.16 | convolution fusion | flops 6712524800 | bytes 13762560 | tf_op jit(solution)/shard_map/tf,td->fd/dot_general | solution.py:121
  572.8 20.2 %fusion.1 = bf16[2,1280,1280]{1,2,0:T(8,128)(2,1)} fusion(bf16[1,2048,1280]{2,1,0:T(8,128)(2,1)} %get-tuple-element.46, bf16[1,2048,1280]{2,1,0:T(8,128)(2,1)} %get-tuple-element.45, bf16[2048,1280]{1,0:T(8,128)(2,1)} %all-gather.7.cloned.1.call-done), kind=kOutput, calls=%fused_computation.13 | convolution fusion | flops 13430292480 | bytes 22282240 | tf_op jit(solution)/shard_map/td,ctf->cdf/dot_general | solution.py:128
  595.9 6.5 fusion.20
  602.5 9.5 reduce-scatter.11.cloned.1.call-done
  617.7 44.2 %all-reduce = (f32[]{:T(128)}, f32[1280]{0:T(1024)S(1)}, f32[1280]{0:T(1024)S(1)}, f32[3,1280]{1,0:T(4,128)S(1)}) all-reduce(f32[]{:T(128)} %get-tuple-element.39, f32[1280]{0:T(1024)S(1)} %get-tuple-element.29, f32[1280]{0:T(1024)S(1)} %get-tuple-element.27, f32[3,1280]{1,0:T(4,128)S(1)} %fusion.49), channel_id=1, replica_groups=mesh['dp'=8,'mp'=4] {'dp','mp'}, use_global_device_ids=true, to_apply=%region_13.14 | all-reduce | flops 6401 | bytes 51208 | tf_op jit(solution)/shard_map/psum | solution.py:175
  664.4 365.7 %all-reduce.4.cloned.1.call-done = (bf16[3,1280,320]{1,2,0:T(8,128)(2,1)}, bf16[320,1280]{1,0:T(8,128)(2,1)}, bf16[2,1280,1280]{1,2,0:T(8,128)(2,1)}, bf16[1280,1280]{1,0:T(8,128)(2,1)}) async-done(((bf16[3,1280,320]{1,2,0:T(8,128)(2,1)}, bf16[320,1280]{1,0:T(8,128)(2,1)}, bf16[2,1280,1280]{1,2,0:T(8,128)(2,1)}, bf16[1280,1280]{1,0:T(8,128)(2,1)}), (bf16[3,1280,320]{1,2,0:T(8,128)(2,1)}, ...) | async-done | bytes 13107216 | tf_op jit(solution)/shard_map/psum | solution.py:179
  1036.0 3.7 convert_multiply_fusion.1
  1040.7 5.8 convert_multiply_fusion
  1046.5 13.9 %copy.54 = f32[2,1280,1280]{2,1,0:T(8,128)} copy(f32[2,1280,1280]{1,2,0:T(8,128)} %convert_multiply_fusion) | data formatting | bytes 26214400
  (154 shorter events, 65.1 us)
Async XLA Ops:
  7.2 4.1 copy-start.31
  7.2 49.1 %all-gather.5.cloned.1.call-start = ((), (), s32[]{:S(2)}) async-start(), calls=%async_computation.4 | async-start | bytes 6553600 | tf_op jit(solution)/shard_map/all_gather | solution.py:85
  8.1 4.9 copy-start.35
  11.3 190.5 %copy-start.4 = (f32[512,1280]{1,0:T(8,128)}, f32[512,1280]{1,0:T(8,128)S(1)}, u32[]{:S(2)}) copy-start(f32[512,1280]{1,0:T(8,128)S(1)} %get-tuple-element.73) | copy-start | bytes 7864324
  11.3 1.8 copy-start.37
  11.3 1.8 copy-start.33
  13.0 188.8 %reduce-scatter.5.cloned.1.call-start = ((), (), s32[]{:S(2)}) async-start(), calls=%async_computation.5 | async-start | bytes 6553600 | tf_op jit(solution)/shard_map/reduce_scatter | solution.py:102
  127.9 3.3 copy-start.8
  127.9 3.3 copy-start.10
  127.9 3.3 copy-start.12
  127.9 3.3 copy-start.14
  131.2 4.3 copy-start.2
  131.2 3.1 copy-start.20
  150.2 54.8 %copy-start.30 = (f32[1280]{0:T(1024)S(1)}, f32[1280]{0:T(1024)}, u32[]{:S(2)}) copy-start(f32[1280]{0:T(1024)} %param.16) | copy-start | bytes 15364
  150.2 96.8 %all-gather.7.cloned.1.call-start = ((), (), s32[]{:S(2)}) async-start(), calls=%async_computation.6 | async-start | bytes 6553600 | tf_op jit(solution)/shard_map/all_gather | solution.py:106
  203.6 3.7 copy-start.18
  206.4 83.1 %all-gather.9.cloned.1.call-start = ((), (), s32[]{:S(2)}) async-start(), calls=%async_computation.8 | async-start | bytes 6553600 | tf_op jit(solution)/shard_map/all_gather | solution.py:120
  208.5 176.0 %reduce-scatter.9.cloned.1.call-start = ((), (), s32[]{:S(2)}) async-start(), calls=%async_computation.9 | async-start | bytes 6553600 | tf_op jit(solution)/shard_map/reduce_scatter | solution.py:134
  333.0 105.4 %reduce-scatter.7.cloned.1.call-start = ((), (), s32[]{:S(2)}) async-start(), calls=%async_computation.7 | async-start | bytes 6553600 | tf_op jit(solution)/shard_map/reduce_scatter | solution.py:116
  345.4 39.1 %copy-start.7 = (f32[512,1280]{1,0:T(8,128)S(1)}, f32[512,1280]{1,0:T(8,128)}, u32[]{:S(2)}) copy-start(f32[512,1280]{1,0:T(8,128)} %copy-done.6) | copy-start | bytes 7864324
  345.4 139.9 %all-gather.11.cloned.1.call-start = ((), (), s32[]{:S(2)}) async-start(), calls=%async_computation.10 | async-start | bytes 6553600 | tf_op jit(solution)/shard_map/all_gather | solution.py:139
  444.7 167.3 %reduce-scatter.11.cloned.1.call-start = ((), (), s32[]{:S(2)}) async-start(), calls=%async_computation.11 | async-start | bytes 6553600 | tf_op jit(solution)/shard_map/reduce_scatter | solution.py:169
  497.8 4.5 copy-start.3
  497.8 4.5 copy-start.21
  503.7 2.2 copy-start.15
  505.9 2.2 copy-start.11
  508.1 1.8 copy-start.19
  508.1 1.8 copy-start.24
  545.5 2.9 copy-start.23
  548.5 1.9 copy-start.28
  560.4 469.8 %all-reduce.4.cloned.1.call-start = ((), (), s32[]{:S(2)}) async-start(), calls=%async_computation.12 | async-start | bytes 26214400 | tf_op jit(solution)/shard_map/psum | solution.py:179
  560.4 32.6 %slice-start.4 = ((s8[5242880]{0:T(1024)(128)(4,1)}), s8[4194304]{0:T(1024)(128)(4,1)S(1)}, s32[]{:S(2)}) async-start(s8[5242880]{0:T(1024)(128)(4,1)} %bitcast.110), calls=%async_computation.17 | async-start | bytes 8388608
  560.5 35.5 %slice-start.2 = ((s8[5242880]{0:T(1024)(128)(4,1)}), s8[4194304]{0:T(1024)(128)(4,1)S(1)}, s32[]{:S(2)}) async-start(s8[5242880]{0:T(1024)(128)(4,1)} %bitcast.108), calls=%async_computation.15 | async-start | bytes 8388608
  572.8 20.3 %copy-start.27 = (bf16[2048,320]{1,0:T(8,128)(2,1)S(1)}, bf16[2048,320]{1,0:T(8,128)(2,1)}, u32[]{:S(2)}) copy-start(bf16[2048,320]{1,0:T(8,128)(2,1)} %convert_element_type.131) | copy-start | bytes 3932164
  572.8 20.3 %slice-start.5 = ((s8[5242880]{0:T(1024)(128)(4,1)}), s8[1048576]{0:T(1024)(128)(4,1)S(1)}, s32[]{:S(2)}) async-start(s8[5242880]{0:T(1024)(128)(4,1)} %bitcast.110), calls=%async_computation.18 | async-start | bytes 2097152
  572.8 23.1 %slice-start.3 = ((s8[5242880]{0:T(1024)(128)(4,1)}), s8[1048576]{0:T(1024)(128)(4,1)S(1)}, s32[]{:S(2)}) async-start(s8[5242880]{0:T(1024)(128)(4,1)} %bitcast.108), calls=%async_computation.16 | async-start | bytes 2097152
  593.1 2.8 copy-start.29
  602.5 9.5 copy-start.5
  602.5 9.5 copy-start.32
  602.5 9.5 copy-start.34
  612.0 2.3 copy-start.17
  612.0 2.5 copy-start.22
  614.5 2.2 copy-start.36
  1030.2 2.6 copy-start.26
  1032.7 3.3 copy-start.25
  1032.7 7.0 slice-start
  1036.0 4.7 slice-start.1
  1046.5 13.9 %copy-start.1 = (f32[3,1280]{1,0:T(4,128)S(1)}, f32[3,1280]{1,0:T(4,128)}, u32[]{:S(2)}) copy-start(f32[3,1280]{1,0:T(4,128)} %param.14) | copy-start | bytes 46084
  (5 other events, 7.1 us)
Sparse Core Ops, SparseCore 0:
  13.1 43.1 all-gather.4
  150.3 51.3 reduce-scatter.4
  206.5 40.4 all-gather.6
  249.1 40.4 all-gather.8
  333.1 51.3 reduce-scatter.8
  386.9 51.3 reduce-scatter.6
  444.8 40.4 all-gather.10
  560.5 51.3 reduce-scatter.10
  617.3 412.7 all-reduce.3
where the time goes:
time: 1080 us; the launch traced here: 1070 us
  waiting for transfers between devices  653 us (60%)
  matrix products  168 us (16%)
  local copies, waits for them, and re-layouts  122 us (11%)
  other arithmetic  63.7 us (6%)
  blocking collectives  44.2 us (4%)
  between operations  15.3 us (1%)
    psum x1, waiting for transfers between devices, body(): lax.psum(grad_qkv.astype(jnp.bfloat16), 'dp').astype(jnp.float32)  366 us
    reduce_scatter x1, waiting for transfers between devices, body(): lax.psum_scatter(mlp_part.astype(jnp.bfloat16), 'mp', scatter_dimension=0...  51.7 us
    reduce_scatter x1, waiting for transfers between devices, body(): lax.psum_scatter(attn_part.astype(jnp.bfloat16), 'mp', scatter_dimension=...  51.5 us
    unnamed x95, local copies, waits for them, and re-layouts  46.5 us
    psum x1, blocking collectives, body(): lax.psum((grad_gain_attn, grad_gain_mlp, grad_table, jnp.sum(mine_valid))...  44.2 us
    all_gather x1, waiting for transfers between devices, body(): lax.all_gather(grad_after.astype(jnp.bfloat16), 'mp', axis=0, tiled=True)  40.5 us
    reduce_scatter x1, waiting for transfers between devices, body(): lax.psum_scatter(mlp_back_part.astype(jnp.bfloat16), 'mp', scatter_dimens...  39.1 us
    all_gather x1, waiting for transfers between devices, body(): normed_mlp = lax.all_gather(normed_mlp_mine, 'mp', axis=0, tiled=True)  38.5 us
  transfers between devices with their start and end apart: 9, of which 9 were waited for; matrix products, arithmetic and copies ran while one was open for 9% of the time, Pallas kernels for 0%

commit v1 on v0

--- a/solution.py
+++ b/solution.py
@@ -68,6 +68,10 @@
     w_down,
     cotangent,
 ):
+
+    def answer_copies(x_in, axis_name, lane_axis):
+        return lax.psum(lax.psum(x_in, axis_name), axis_name=lane_axis)
+
     local_rows = rows.shape[0]
     mp_index = lax.axis_index("mp")
     series_count = lengths.shape[0]
@@ -172,8 +176,8 @@
     grad_rows_attn, grad_gain_attn = norm_backward(start_rows, inverse_attn, gain_attn, grad_normed)
     grad_rows = grad_after + grad_rows_attn
     grad_table = jnp.dot(onehot.T, grad_rows, precision=HIGHEST)
-    grad_gain_attn, grad_gain_mlp, grad_table, token_total = lax.psum(
-        (grad_gain_attn, grad_gain_mlp, grad_table, jnp.sum(mine_valid)), ("dp", "mp")
+    grad_gain_attn, grad_gain_mlp, grad_table, token_total = answer_copies(
+        (grad_gain_attn, grad_gain_mlp, grad_table, jnp.sum(mine_valid)), "mp", "dp"
     )
     grad_qkv, grad_out, grad_gate_up, grad_down = (
         lax.psum(grad_qkv.astype(jnp.bfloat16), "dp").astype(jnp.float32),

time: 1080 us -> 1080 us (level)
    psum x1 -> x2, blocking collectives: 44.2 us -> 53.6 us  [answer_copies(): return lax.psum(lax.psum(x_in, axis_name), axis_name=lane_axis)]
where the time goes in v1:
time: 1080 us; the launch traced here: 1070 us
  waiting for transfers between devices  644 us (60%)
  matrix products  169 us (16%)
  local copies, waits for them, and re-layouts  122 us (11%)
  other arithmetic  63.7 us (6%)
  blocking collectives  53.6 us (5%)
  between operations  15.3 us (1%)
    psum x1, waiting for transfers between devices, body(): lax.psum(grad_qkv.astype(jnp.bfloat16), 'dp').astype(jnp.float32)  357 us
    psum x2, blocking collectives, answer_copies(): return lax.psum(lax.psum(x_in, axis_name), axis_name=lane_axis)  53.6 us
    reduce_scatter x1, waiting for transfers between devices, body(): lax.psum_scatter(mlp_part.astype(jnp.bfloat16), 'mp', scatter_dimension=0...  51.7 us
    reduce_scatter x1, waiting for transfers between devices, body(): lax.psum_scatter(attn_part.astype(jnp.bfloat16), 'mp', scatter_dimension=...  51.5 us
    unnamed x95, local copies, waits for them, and re-layouts  46.5 us
    all_gather x1, waiting for transfers between devices, body(): lax.all_gather(grad_after.astype(jnp.bfloat16), 'mp', axis=0, tiled=True)  40.5 us
    reduce_scatter x1, waiting for transfers between devices, body(): lax.psum_scatter(mlp_back_part.astype(jnp.bfloat16), 'mp', scatter_dimens...  39.1 us
    all_gather x1, waiting for transfers between devices, body(): normed_mlp = lax.all_gather(normed_mlp_mine, 'mp', axis=0, tiled=True)  38.5 us
  transfers between devices with their start and end apart: 9, of which 9 were waited for; matrix products, arithmetic and copies ran while one was open for 9% of the time, Pallas kernels for 0%

profile of v1, /device:TPU:0, one launch (start us, length us, event | category | flops | bytes accessed | tf_op | source)
XLA Modules:
  0.0 1067.4 jit_solution(10487443622468101147)
XLA Ops:
  13.6 5.8 fusion.48
  19.4 36.9 %all-gather.5.cloned.1.call-done = bf16[2048,1280]{1,0:T(8,128)(2,1)} async-done(((bf16[512,1280]{1,0:T(8,128)(2,1)}), bf16[2048,1280]{1,0:T(8,128)(2,1)}) %all-gather.5.cloned.1.call-update) | async-done | bytes 5242896 | tf_op jit(solution)/shard_map/all_gather | solution.py:89
  56.3 8.7 fusion.10
  69.2 4.9 reshape.176
  74.1 4.7 copy.39
  78.8 5.3 reshape.177
  84.1 5.5 fusion.62
  89.6 4.9 copy.73
  94.4 4.9 copy.72
  99.3 5.3 reshape.178
  104.7 5.5 fusion.63
  110.1 4.9 copy.75
  115.0 4.9 copy.74
  119.9 7.9 subtract_convert_fusion.3
  135.5 3.3 copy.41
  138.7 4.3 convert_element_type.131
  143.1 7.1 convolution_convert_fusion.2
  150.3 51.5 %reduce-scatter.5.cloned.1.call-done = bf16[512,1280]{1,0:T(8,128)(2,1)} async-done(((bf16[2048,1280]{1,0:T(8,128)(2,1)}), bf16[512,1280]{1,0:T(8,128)(2,1)}) %reduce-scatter.5.cloned.1.call-update) | async-done | bytes 1310736 | tf_op jit(solution)/shard_map/reduce_scatter | solution.py:106
  208.6 38.5 %all-gather.7.cloned.1.call-done = bf16[2048,1280]{1,0:T(8,128)(2,1)} async-done(((bf16[512,1280]{1,0:T(8,128)(2,1)}), bf16[2048,1280]{1,0:T(8,128)(2,1)}) %all-gather.7.cloned.1.call-update) | async-done | bytes 5242896 | tf_op jit(solution)/shard_map/all_gather | solution.py:110
  247.0 22.7 %convolution_bitcast_fusion = f32[2,2048,1280]{2,1,0:T(8,128)} fusion(bf16[2048,1280]{1,0:T(8,128)(2,1)} %all-gather.7.cloned.1.call-done, f32[2,1280,1280]{2,1,0:T(8,128)} %param.19), kind=kOutput, calls=%fused_computation.1 | convolution fusion | flops 13425049600 | bytes 39321600 | tf_op jit(solution)/shard_map/td,cdf->ctf/dot_general | solution.py:112
  269.7 19.9 %all-gather.9.cloned.1.call-done = bf16[2048,1280]{1,0:T(8,128)(2,1)} async-done(((bf16[512,1280]{1,0:T(8,128)(2,1)}), bf16[2048,1280]{1,0:T(8,128)(2,1)}) %all-gather.9.cloned.1.call-update) | async-done | bytes 5242896 | tf_op jit(solution)/shard_map/all_gather | solution.py:124
  289.6 21.7 %fusion.9 = (bf16[1,2048,1280]{2,1,0:T(8,128)(2,1)}, bf16[1,2048,1280]{2,1,0:T(8,128)(2,1)}, bf16[2048,1280]{1,0:T(8,128)(2,1)}) fusion(f32[2,2048,1280]{2,1,0:T(8,128)} %convolution_bitcast_fusion, bf16[2048,1280]{1,0:T(8,128)(2,1)} %all-gather.9.cloned.1.call-done, f32[1280,1280]{1,0:T(8,128)} %param.20), kind=kOutput, calls=%fused_computation.25 | convolution fusion | flops 6751846400 | bytes 48496640 | tf_op jit(solution)/shard_map/td,fd->tf/dot_general | solution.py:126
  311.2 21.7 %bitcast_convert_fusion.1 = bf16[2048,1280]{1,0:T(8,128)(2,1)} fusion(bf16[1,2048,1280]{2,1,0:T(8,128)(2,1)} %get-tuple-element.50, bf16[1,2048,1280]{2,1,0:T(8,128)(2,1)} %get-tuple-element.49, f32[2,1280,1280]{2,1,0:T(8,128)} %param.19), kind=kOutput, calls=%fused_computation.7 | convolution fusion | flops 13432913920 | bytes 28835840 | tf_op jit(solution)/shard_map/ctf,cdf->td/dot_general | solution.py:135
  333.0 12.3 %convolution_convert_fusion.1 = bf16[2048,1280]{1,0:T(8,128)(2,1)} fusion(bf16[2048,1280]{1,0:T(8,128)(2,1)} %get-tuple-element.51, f32[1280,1280]{1,0:T(8,128)} %param.20), kind=kOutput, calls=%fused_computation.14 | convolution fusion | flops 6715146240 | bytes 17039360 | tf_op jit(solution)/shard_map/dot_general | solution.py:119
  345.4 39.1 %reduce-scatter.9.cloned.1.call-done = bf16[512,1280]{1,0:T(8,128)(2,1)} async-done(((bf16[2048,1280]{1,0:T(8,128)(2,1)}), bf16[512,1280]{1,0:T(8,128)(2,1)}) %reduce-scatter.9.cloned.1.call-update) | async-done | bytes 1310736 | tf_op jit(solution)/shard_map/reduce_scatter | solution.py:138
  386.7 51.7 %reduce-scatter.7.cloned.1.call-done = bf16[512,1280]{1,0:T(8,128)(2,1)} async-done(((bf16[2048,1280]{1,0:T(8,128)(2,1)}), bf16[512,1280]{1,0:T(8,128)(2,1)}) %reduce-scatter.7.cloned.1.call-update) | async-done | bytes 1310736 | tf_op jit(solution)/shard_map/reduce_scatter | solution.py:120
  438.3 6.3 fusion.59
  444.7 40.5 %all-gather.11.cloned.1.call-done = bf16[2048,1280]{1,0:T(8,128)(2,1)} async-done(((bf16[512,1280]{1,0:T(8,128)(2,1)}), bf16[2048,1280]{1,0:T(8,128)(2,1)}) %all-gather.11.cloned.1.call-update) | async-done | bytes 5242896 | tf_op jit(solution)/shard_map/all_gather | solution.py:143
  485.3 4.9 convolution_convert_fusion.5
  490.2 4.0 reshape.179
  494.1 3.6 copy.43
  497.8 4.5 convert_bitcast_fusion
  509.9 4.7 subtract_convert_fusion
  517.1 5.0 copy.59
  525.1 5.0 copy.60
  533.0 4.7 pad_maximum_fusion.5
  537.7 5.0 copy.58
  550.5 9.9 bitcast_convert_fusion
  560.5 12.3 %convolution_convert_fusion.3 = bf16[1280,1280]{1,0:T(8,128)(2,1)} fusion(bf16[2048,1280]{1,0:T(8,128)(2,1)} %get-tuple-element.51, bf16[2048,1280]{1,0:T(8,128)(2,1)} %all-gather.9.cloned.1.call-done), kind=kOutput, calls=%fused_computation.16 | convolution fusion | flops 6712524800 | bytes 13762560 | tf_op jit(solution)/shard_map/tf,td->fd/dot_general | solution.py:125
  572.8 20.2 %fusion.1 = bf16[2,1280,1280]{1,2,0:T(8,128)(2,1)} fusion(bf16[1,2048,1280]{2,1,0:T(8,128)(2,1)} %get-tuple-element.50, bf16[1,2048,1280]{2,1,0:T(8,128)(2,1)} %get-tuple-element.49, bf16[2048,1280]{1,0:T(8,128)(2,1)} %all-gather.7.cloned.1.call-done), kind=kOutput, calls=%fused_computation.13 | convolution fusion | flops 13430292480 | bytes 22282240 | tf_op jit(solution)/shard_map/td,ctf->cdf/dot_general | solution.py:132
  595.9 6.5 fusion.20
  602.5 9.4 reduce-scatter.11.cloned.1.call-done
  617.7 11.9 %all-reduce.1 = (f32[]{:T(128)}, f32[1280]{0:T(1024)S(1)}, f32[1280]{0:T(1024)S(1)}, f32[3,1280]{1,0:T(4,128)S(1)}) all-reduce(f32[]{:T(128)} %get-tuple-element.43, f32[1280]{0:T(1024)S(1)} %get-tuple-element.29, f32[1280]{0:T(1024)S(1)} %get-tuple-element.27, f32[3,1280]{1,0:T(4,128)S(1)} %fusion.49), channel_id=1, replica_groups=mesh['dp'=8,'mp'=4] {'mp'}, use_global_device_ids=true, to_apply=%region_13.14 | all-reduce | flops 6401 | bytes 51208 | tf_op jit(solution)/shard_map/psum | solution.py:73
  629.6 41.7 %all-reduce = (f32[]{:T(128)}, f32[1280]{0:T(1024)S(1)}, f32[1280]{0:T(1024)S(1)}, f32[3,1280]{1,0:T(4,128)S(1)}) all-reduce(f32[]{:T(128)} %get-tuple-element.35, f32[1280]{0:T(1024)S(1)} %get-tuple-element.36, f32[1280]{0:T(1024)S(1)} %get-tuple-element.37, f32[3,1280]{1,0:T(4,128)S(1)} %get-tuple-element.38), channel_id=1, replica_groups=mesh['dp'=8,'mp'=4] {'dp'}, use_global_device_ids=true, to_apply=%region_14.15 | all-reduce | flops 6401 | bytes 51208 | tf_op jit(solution)/shard_map/psum | solution.py:73
  673.8 356.6 %all-reduce.5.cloned.1.call-done = (bf16[3,1280,320]{1,2,0:T(8,128)(2,1)}, bf16[320,1280]{1,0:T(8,128)(2,1)}, bf16[2,1280,1280]{1,2,0:T(8,128)(2,1)}, bf16[1280,1280]{1,0:T(8,128)(2,1)}) async-done(((bf16[3,1280,320]{1,2,0:T(8,128)(2,1)}, bf16[320,1280]{1,0:T(8,128)(2,1)}, bf16[2,1280,1280]{1,2,0:T(8,128)(2,1)}, bf16[1280,1280]{1,0:T(8,128)(2,1)}), (bf16[3,1280,320]{1,2,0:T(8,128)(2,1)}, ...) | async-done | bytes 13107216 | tf_op jit(solution)/shard_map/psum | solution.py:183
  1036.2 3.7 convert_multiply_fusion.1
  1041.0 5.8 convert_multiply_fusion
  1046.8 13.9 %copy.54 = f32[2,1280,1280]{2,1,0:T(8,128)} copy(f32[2,1280,1280]{1,2,0:T(8,128)} %convert_multiply_fusion) | data formatting | bytes 26214400
  (155 shorter events, 68.3 us)
Async XLA Ops:
  7.2 4.1 copy-start.31
  7.2 49.1 %all-gather.5.cloned.1.call-start = ((), (), s32[]{:S(2)}) async-start(), calls=%async_computation.4 | async-start | bytes 6553600 | tf_op jit(solution)/shard_map/all_gather | solution.py:89
  8.1 4.9 copy-start.35
  11.3 190.5 %copy-start.4 = (f32[512,1280]{1,0:T(8,128)}, f32[512,1280]{1,0:T(8,128)S(1)}, u32[]{:S(2)}) copy-start(f32[512,1280]{1,0:T(8,128)S(1)} %get-tuple-element.77) | copy-start | bytes 7864324
  11.3 1.8 copy-start.37
  11.3 1.8 copy-start.33
  13.0 188.8 %reduce-scatter.5.cloned.1.call-start = ((), (), s32[]{:S(2)}) async-start(), calls=%async_computation.5 | async-start | bytes 6553600 | tf_op jit(solution)/shard_map/reduce_scatter | solution.py:106
  127.9 3.3 copy-start.8
  127.9 3.3 copy-start.10
  127.9 3.3 copy-start.12
  127.9 3.3 copy-start.14
  131.2 4.3 copy-start.2
  131.2 3.1 copy-start.20
  150.2 54.8 %copy-start.30 = (f32[1280]{0:T(1024)S(1)}, f32[1280]{0:T(1024)}, u32[]{:S(2)}) copy-start(f32[1280]{0:T(1024)} %param.16) | copy-start | bytes 15364
  150.2 96.8 %all-gather.7.cloned.1.call-start = ((), (), s32[]{:S(2)}) async-start(), calls=%async_computation.6 | async-start | bytes 6553600 | tf_op jit(solution)/shard_map/all_gather | solution.py:110
  203.6 3.7 copy-start.18
  206.4 83.1 %all-gather.9.cloned.1.call-start = ((), (), s32[]{:S(2)}) async-start(), calls=%async_computation.8 | async-start | bytes 6553600 | tf_op jit(solution)/shard_map/all_gather | solution.py:124
  208.5 176.0 %reduce-scatter.9.cloned.1.call-start = ((), (), s32[]{:S(2)}) async-start(), calls=%async_computation.9 | async-start | bytes 6553600 | tf_op jit(solution)/shard_map/reduce_scatter | solution.py:138
  333.0 105.4 %reduce-scatter.7.cloned.1.call-start = ((), (), s32[]{:S(2)}) async-start(), calls=%async_computation.7 | async-start | bytes 6553600 | tf_op jit(solution)/shard_map/reduce_scatter | solution.py:120
  345.4 39.2 %copy-start.7 = (f32[512,1280]{1,0:T(8,128)S(1)}, f32[512,1280]{1,0:T(8,128)}, u32[]{:S(2)}) copy-start(f32[512,1280]{1,0:T(8,128)} %copy-done.6) | copy-start | bytes 7864324
  345.4 139.9 %all-gather.11.cloned.1.call-start = ((), (), s32[]{:S(2)}) async-start(), calls=%async_computation.10 | async-start | bytes 6553600 | tf_op jit(solution)/shard_map/all_gather | solution.py:143
  444.7 167.3 %reduce-scatter.11.cloned.1.call-start = ((), (), s32[]{:S(2)}) async-start(), calls=%async_computation.11 | async-start | bytes 6553600 | tf_op jit(solution)/shard_map/reduce_scatter | solution.py:173
  497.8 4.5 copy-start.3
  497.8 4.5 copy-start.21
  503.7 2.2 copy-start.15
  505.9 2.2 copy-start.11
  508.1 1.8 copy-start.19
  508.1 1.8 copy-start.24
  545.5 2.9 copy-start.23
  548.6 1.9 copy-start.28
  560.4 470.0 %all-reduce.5.cloned.1.call-start = ((), (), s32[]{:S(2)}) async-start(), calls=%async_computation.12 | async-start | bytes 26214400 | tf_op jit(solution)/shard_map/psum | solution.py:183
  560.4 32.6 %slice-start.4 = ((s8[5242880]{0:T(1024)(128)(4,1)}), s8[4194304]{0:T(1024)(128)(4,1)S(1)}, s32[]{:S(2)}) async-start(s8[5242880]{0:T(1024)(128)(4,1)} %bitcast.110), calls=%async_computation.17 | async-start | bytes 8388608
  560.5 35.5 %slice-start.2 = ((s8[5242880]{0:T(1024)(128)(4,1)}), s8[4194304]{0:T(1024)(128)(4,1)S(1)}, s32[]{:S(2)}) async-start(s8[5242880]{0:T(1024)(128)(4,1)} %bitcast.108), calls=%async_computation.15 | async-start | bytes 8388608
  572.8 20.3 %copy-start.27 = (bf16[2048,320]{1,0:T(8,128)(2,1)S(1)}, bf16[2048,320]{1,0:T(8,128)(2,1)}, u32[]{:S(2)}) copy-start(bf16[2048,320]{1,0:T(8,128)(2,1)} %convert_element_type.131) | copy-start | bytes 3932164
  572.8 20.3 %slice-start.5 = ((s8[5242880]{0:T(1024)(128)(4,1)}), s8[1048576]{0:T(1024)(128)(4,1)S(1)}, s32[]{:S(2)}) async-start(s8[5242880]{0:T(1024)(128)(4,1)} %bitcast.110), calls=%async_computation.18 | async-start | bytes 2097152
  572.8 23.1 %slice-start.3 = ((s8[5242880]{0:T(1024)(128)(4,1)}), s8[1048576]{0:T(1024)(128)(4,1)S(1)}, s32[]{:S(2)}) async-start(s8[5242880]{0:T(1024)(128)(4,1)} %bitcast.108), calls=%async_computation.16 | async-start | bytes 2097152
  593.1 2.8 copy-start.29
  602.5 9.5 copy-start.5
  602.5 9.5 copy-start.32
  602.5 9.5 copy-start.34
  612.0 2.3 copy-start.17
  612.0 2.5 copy-start.22
  614.5 2.2 copy-start.36
  1030.4 2.6 copy-start.26
  1032.9 3.3 copy-start.25
  1033.0 7.0 slice-start
  1036.2 4.7 slice-start.1
  1046.8 13.9 %copy-start.1 = (f32[3,1280]{1,0:T(4,128)S(1)}, f32[3,1280]{1,0:T(4,128)}, u32[]{:S(2)}) copy-start(f32[3,1280]{1,0:T(4,128)} %param.14) | copy-start | bytes 46084
  (5 other events, 7.1 us)
Sparse Core Ops, SparseCore 0:
  13.1 43.1 all-gather.4
  150.4 51.3 reduce-scatter.4
  206.5 40.4 all-gather.6
  249.1 40.4 all-gather.8
  333.1 51.3 reduce-scatter.8
  386.9 51.3 reduce-scatter.6
  444.8 40.4 all-gather.10
  560.5 51.3 reduce-scatter.10
  617.3 412.9 all-reduce.4
